TPU v7x, 512 devices: a whole 4x4x16 slice. The times are simulated.
512 devices in a mesh: gx: 16 (over z), gy: 4 (over x), gz: 8 (over y, core).
Axes of the slice: x: 4, y: 4, z: 16, core: 2. Of those that a mesh axis runs over, the one named last changes fastest.
Arguments:
- flow: float32 [4, 128, 64, 1024], P(None, 'gx', 'gy', 'gz'), may hold values from -3 to 3
- basis: float32 [127, 3, 131072], P(None, None, ('gx', 'gy', 'gz')), may hold values from -1150 to 1150
- sample: int32 [131072], P(('gx', 'gy', 'gz')), may hold values from 0 to 16383
Outputs:
- flow_next: float32 [4, 128, 64, 1024], P(None, 'gx', 'gy', 'gz')
- basis_next: float32 [128, 3, 131072], P(None, None, ('gx', 'gy', 'gz'))
- factor: float32 [128, 128], replicated
All inputs are finite; a program needn't handle non-finite values.
Results may differ from a plain program's by a relative error of at most 0.000065.
Values sent between devices are 32-bit elements; how exact they have to be, the bound alone decides.
A program may use at most 64 MiB of HBM per device.

v0:
```python
import jax
import jax.numpy as jnp
from jax import lax
from jax.sharding import PartitionSpec as P

DT_STEP = 0.35
VISCOSITY = 0.2
SOUND_SQ = 1.0
DRIVING = 0.5


def padded(block, sides, width, periodic):
    for axis, dim in sides:
        count = lax.axis_size(axis)
        forward = [(i, i + 1) for i in range(count - 1)]
        if periodic:
            forward.append((count - 1, 0))
        backward = [(target, source) for source, target in forward]
        low = lax.ppermute(
            lax.slice_in_dim(block, block.shape[dim] - width, None, axis=dim), axis, forward
        )
        high = lax.ppermute(lax.slice_in_dim(block, 0, width, axis=dim), axis, backward)
        block = jnp.concatenate([low, block, high], axis=dim)
    return block


def rates(ext):
    centre = ext[:, 1:-1, 1:-1, 1:-1]
    x_plus = ext[:, 2:, 1:-1, 1:-1]
    x_minus = ext[:, :-2, 1:-1, 1:-1]
    y_plus = ext[:, 1:-1, 2:, 1:-1]
    y_minus = ext[:, 1:-1, :-2, 1:-1]
    z_plus = ext[:, 1:-1, 1:-1, 2:]
    z_minus = ext[:, 1:-1, 1:-1, :-2]
    slope_x = 0.5 * (x_plus - x_minus)
    slope_y = 0.5 * (y_plus - y_minus)
    slope_z = 0.5 * (z_plus - z_minus)
    laplace = x_plus + x_minus + (y_plus + y_minus) + (z_plus + z_minus) - 6.0 * centre
    advect = centre[0] * slope_x[:3] + centre[1] * slope_y[:3] + centre[2] * slope_z[:3]
    pressure = jnp.stack([slope_x[3], slope_y[3], slope_z[3]])
    forcing = jnp.array([DRIVING, 0.0, 0.0], dtype=jnp.float32).reshape(3, 1, 1, 1)
    velocity = VISCOSITY * laplace[:3] - advect - pressure + forcing
    density = -SOUND_SQ * (slope_x[0] + slope_y[1] + slope_z[2])
    return jnp.concatenate([velocity, density[None]], axis=0)


def extend_one(fields):
    walled = padded(fields, (("gy", 2),), 1, False)
    return padded(walled, (("gx", 1), ("gz", 3)), 1, True)


def local(flow, basis, sample):
    points = basis.shape[2]
    modes = basis.shape[0]
    count = 3.0 * points * lax.axis_size("gx") * lax.axis_size("gy") * lax.axis_size("gz")
    section_one = flow + DT_STEP * rates(extend_one(flow))
    section_two = 0.75 * flow + 0.25 * (section_one + DT_STEP * rates(extend_one(section_one)))
    flow_next = 1.0 / 3.0 * flow + 2.0 / 3.0 * (
        section_two + DT_STEP * rates(extend_one(section_two))
    )
    velocity = flow_next[:3].reshape(3, -1)
    snapshot = jnp.take(velocity, sample, axis=1)
    stacked = jnp.concatenate([basis, snapshot[None]], axis=0).reshape(modes + 1, 3 * points)
    local_gram = jnp.dot(
        stacked, stacked.T, precision=lax.Precision.HIGHEST, preferred_element_type=jnp.float32
    )
    gram = lax.psum(local_gram, ("gx", "gy", "gz")) / count
    lower = jnp.linalg.cholesky(gram)
    basis_next = jax.scipy.linalg.solve_triangular(lower, stacked, lower=True).reshape(
        modes + 1, 3, points
    )
    return (flow_next, basis_next, lower.T)


def solution(mesh):
    return jax.shard_map(
        local,
        mesh=mesh,
        in_specs=(
            P(None, "gx", "gy", "gz"),
            P(None, None, ("gx", "gy", "gz")),
            P(("gx", "gy", "gz")),
        ),
        out_specs=(P(None, "gx", "gy", "gz"), P(None, None, ("gx", "gy", "gz")), P()),
        check_vma=False,
    )
```

profile of v0, /device:TPU:1, one launch (start us, length us, event | category | flops | bytes accessed | tf_op | source)
XLA Modules:
  0.0 582.4 jit_solution(7620865436270588193)
XLA Ops:
  8.3 3.9 collective-permute-start
  14.4 2.2 collective-permute-done.1
  17.5 11.1 %collective-permute-start.2 = (f32[4,1,18,128]{3,2,1,0:T(8,128)S(1)}, f32[4,1,18,128]{3,2,1,0:T(8,128)S(1)}, u32[]{:S(2)}, u32[]{:S(2)}) collective-permute-start(f32[4,1,18,128]{3,2,1,0:T(8,128)S(1)} %get-tuple-element.41), channel_id=1, source_target_pairs={{32,0},{64,32},{96,64},{128,96},{160,128},{192,160},{224,192},{256... | collective-permute-start | bytes 110600 | tf_op jit(solution)/shard_map/ppermute | solution.py:22
  28.6 1.9 collective-permute-start.3
  31.2 3.4 collective-permute-done.3
  35.9 3.5 collective-permute-start.4
  42.2 5.2 collective-permute-done.4
  50.4 3.1 collective-permute-start.6
  54.9 3.1 collective-permute-done.7
  60.0 3.4 collective-permute-start.9
  63.4 2.6 collective-permute-done.9
  66.3 4.2 collective-permute-start.10
  70.7 6.5 %collective-permute-done.10 = f32[4,10,18,1]{3,2,1,0:T(8,128)S(1)} collective-permute-done((f32[4,10,18,1]{3,2,1,0:T(8,128)S(1)}, f32[4,10,18,1]{3,2,1,0:T(8,128)S(1)}, u32[]{:S(2)}, u32[]{:S(2)}) %collective-permute-start.10) | collective-permute-done | bytes 2912 | tf_op jit(solution)/shard_map/ppermute | solution.py:22
  77.9 2.8 collective-permute-start.12
  82.2 3.0 collective-permute-done.13
  87.1 3.5 collective-permute-start.15
  90.7 2.5 collective-permute-done.15
  93.4 5.4 collective-permute-start.16
  99.0 5.4 collective-permute-done.16
  105.3 4.7 copy.16
  110.1 4.1 gather_fusion
  115.8 433.0 %all-reduce.2.cloned.1.call-done = f32[128,128]{0,1:T(8,128)} async-done(((f32[128,128]{0,1:T(8,128)}), f32[128,128]{0,1:T(8,128)}) %all-reduce.2.cloned.1.call-update) | async-done | bytes 65552 | tf_op jit(solution)/shard_map/psum | solution.py:67
  550.6 11.7 %cholesky.16 = f32[128,128]{1,0:T(8,128)S(1)} custom-call(f32[128,128]{1,0:T(8,128)S(1)} %fusion.57), custom_call_target="Cholesky" | custom-call | tf_op jit(solution)/shard_map/jit(cholesky)/cholesky | solution.py:68
  563.7 9.8 %custom-call.7 = f32[1,128,128]{1,2,0:T(8,128)S(1)} custom-call(f32[1,128,128]{2,1,0:T(8,128)S(1)} %get-tuple-element.70), custom_call_target="InvertDiagBlocksLowerTriangular" | custom-call | tf_op jit(solution)/shard_map/jit(_solve_triangular)/triangular_solve | solution.py:69
  (79 shorter events, 27.4 us)
Async XLA Ops:
  7.2 43.2 %copy-start = (f32[4,8,16,128]{3,2,1,0:T(8,128)S(1)}, f32[4,8,16,128]{3,2,1,0:T(8,128)}, u32[]{:S(2)}) copy-start(f32[4,8,16,128]{3,2,1,0:T(8,128)} %param.6) | copy-start | bytes 786436
  7.2 47.7 %copy-start.4 = (s32[256]{0:T(256)S(1)}, s32[256]{0:T(256)}, u32[]{:S(2)}) copy-start(s32[256]{0:T(256)} %param.8) | copy-start | bytes 3076
  7.2 541.6 %all-reduce.2.cloned.1.call-start = ((), (), s32[]{:S(2)}) async-start(), calls=%async_computation | async-start | bytes 131072 | tf_op jit(solution)/shard_map/psum | solution.py:67
  8.3 6.2 %collective-permute-start = (f32[4,8,1,128]{3,2,1,0:T(1,128)S(1)}, f32[4,8,1,128]{3,2,1,0:T(1,128)S(1)}, u32[]{:S(2)}, u32[]{:S(2)}) collective-permute-start(f32[4,8,1,128]{3,2,1,0:T(1,128)S(1)} %get-tuple-element.67), channel_id=1, source_target_pairs={{0,8},{8,16},{16,24},{1,9},{9,17},{17,25},{2,10},{10,18},{18,26},{... | collective-permute-start | bytes 49160 | tf_op jit(solution)/shard_map/ppermute | solution.py:19
  12.2 4.5 collective-permute-start.1
  17.5 13.7 %collective-permute-start.2 = (f32[4,1,18,128]{3,2,1,0:T(8,128)S(1)}, f32[4,1,18,128]{3,2,1,0:T(8,128)S(1)}, u32[]{:S(2)}, u32[]{:S(2)}) collective-permute-start(f32[4,1,18,128]{3,2,1,0:T(8,128)S(1)} %get-tuple-element.41), channel_id=1, source_target_pairs={{32,0},{64,32},{96,64},{128,96},{160,128},{192,160},{224,192},{256... | collective-permute-start | bytes 110600 | tf_op jit(solution)/shard_map/ppermute | solution.py:22
  28.6 6.0 %collective-permute-start.3 = (f32[4,1,18,128]{3,2,1,0:T(8,128)S(1)}, f32[4,1,18,128]{3,2,1,0:T(8,128)S(1)}, u32[]{:S(2)}, u32[]{:S(2)}) collective-permute-start(f32[4,1,18,128]{3,2,1,0:T(8,128)S(1)} %get-tuple-element.40), channel_id=1, source_target_pairs={{0,32},{32,64},{64,96},{96,128},{128,160},{160,192},{192,224},{224... | collective-permute-start | bytes 110600 | tf_op jit(solution)/shard_map/ppermute | solution.py:19
  35.7 41.9 %copy-start.3 = (f32[3]{0:T(128)S(1)}, f32[3]{0:T(128)}, u32[]{:S(2)}) copy-start(f32[3]{0:T(128)} %constant.80.clone) | copy-start | bytes 40
  35.9 11.5 %collective-permute-start.4 = (f32[4,10,18,1]{3,2,1,0:T(8,128)S(1)}, f32[4,10,18,1]{3,2,1,0:T(8,128)S(1)}, u32[]{:S(2)}, u32[]{:S(2)}) collective-permute-start(f32[4,10,18,1]{3,2,1,0:T(8,128)S(1)} %get-tuple-element.31), channel_id=1, source_target_pairs={{1,0},{2,1},{3,2},{4,3},{5,4},{6,5},{7,6},{0,7},{9,8},{10,9},{11,1... | collective-permute-start | bytes 8648 | tf_op jit(solution)/shard_map/ppermute | solution.py:22
  39.4 8.0 %collective-permute-start.5 = (f32[4,10,18,1]{3,2,1,0:T(8,128)S(1)}, f32[4,10,18,1]{3,2,1,0:T(8,128)S(1)}, u32[]{:S(2)}, u32[]{:S(2)}) collective-permute-start(f32[4,10,18,1]{3,2,1,0:T(8,128)S(1)} %get-tuple-element.32), channel_id=1, source_target_pairs={{0,1},{1,2},{2,3},{3,4},{4,5},{5,6},{6,7},{7,0},{8,9},{9,10},{10,1... | collective-permute-start | bytes 8648 | tf_op jit(solution)/shard_map/ppermute | solution.py:19
  42.2 39.8 %copy-start.1 = (f32[127,3,256]{2,0,1:T(8,128)S(1)}, f32[127,3,256]{2,0,1:T(8,128)}, u32[]{:S(2)}) copy-start(f32[127,3,256]{2,0,1:T(8,128)} %param.7) | copy-start | bytes 1170436
  50.4 4.5 collective-permute-start.6
  53.6 4.5 collective-permute-start.7
  58.1 5.3 collective-permute-start.8
  60.0 6.0 %collective-permute-start.9 = (f32[4,1,18,128]{3,2,1,0:T(8,128)S(1)}, f32[4,1,18,128]{3,2,1,0:T(8,128)S(1)}, u32[]{:S(2)}, u32[]{:S(2)}) collective-permute-start(f32[4,1,18,128]{3,2,1,0:T(8,128)S(1)} %get-tuple-element.37), channel_id=1, source_target_pairs={{0,32},{32,64},{64,96},{96,128},{128,160},{160,192},{192,224},{224... | collective-permute-start | bytes 110600 | tf_op jit(solution)/shard_map/ppermute | solution.py:19
  66.3 10.9 %collective-permute-start.10 = (f32[4,10,18,1]{3,2,1,0:T(8,128)S(1)}, f32[4,10,18,1]{3,2,1,0:T(8,128)S(1)}, u32[]{:S(2)}, u32[]{:S(2)}) collective-permute-start(f32[4,10,18,1]{3,2,1,0:T(8,128)S(1)} %get-tuple-element.29), channel_id=1, source_target_pairs={{1,0},{2,1},{3,2},{4,3},{5,4},{6,5},{7,6},{0,7},{9,8},{10,9},{11,1... | collective-permute-start | bytes 8648 | tf_op jit(solution)/shard_map/ppermute | solution.py:22
  70.5 6.6 %collective-permute-start.11 = (f32[4,10,18,1]{3,2,1,0:T(8,128)S(1)}, f32[4,10,18,1]{3,2,1,0:T(8,128)S(1)}, u32[]{:S(2)}, u32[]{:S(2)}) collective-permute-start(f32[4,10,18,1]{3,2,1,0:T(8,128)S(1)} %get-tuple-element.30), channel_id=1, source_target_pairs={{0,1},{1,2},{2,3},{3,4},{4,5},{5,6},{6,7},{7,0},{8,9},{9,10},{10,1... | collective-permute-start | bytes 8648 | tf_op jit(solution)/shard_map/ppermute | solution.py:19
  77.9 4.3 collective-permute-start.12
  80.7 4.5 collective-permute-start.13
  85.2 5.5 collective-permute-start.14
  87.1 6.0 %collective-permute-start.15 = (f32[4,1,18,128]{3,2,1,0:T(8,128)S(1)}, f32[4,1,18,128]{3,2,1,0:T(8,128)S(1)}, u32[]{:S(2)}, u32[]{:S(2)}) collective-permute-start(f32[4,1,18,128]{3,2,1,0:T(8,128)S(1)} %get-tuple-element.34), channel_id=1, source_target_pairs={{0,32},{32,64},{64,96},{96,128},{128,160},{160,192},{192,224},{224... | collective-permute-start | bytes 110600 | tf_op jit(solution)/shard_map/ppermute | solution.py:19
  93.4 11.0 %collective-permute-start.16 = (f32[4,10,18,1]{3,2,1,0:T(8,128)S(1)}, f32[4,10,18,1]{3,2,1,0:T(8,128)S(1)}, u32[]{:S(2)}, u32[]{:S(2)}) collective-permute-start(f32[4,10,18,1]{3,2,1,0:T(8,128)S(1)} %get-tuple-element.27), channel_id=1, source_target_pairs={{1,0},{2,1},{3,2},{4,3},{5,4},{6,5},{7,6},{0,7},{9,8},{10,9},{11,1... | collective-permute-start | bytes 8648 | tf_op jit(solution)/shard_map/ppermute | solution.py:22
  98.9 5.8 collective-permute-start.17
  105.3 470.2 %copy-start.2 = (f32[4,8,16,128]{3,2,1,0:T(8,128)}, f32[4,8,16,128]{3,2,1,0:T(8,128)S(1)}, u32[]{:S(2)}) copy-start(f32[4,8,16,128]{3,2,1,0:T(8,128)S(1)} %fusion.15) | copy-start | bytes 786436
Sparse Core Ops, SparseCore 0:
  115.5 433.2 all-reduce.1
where the time goes:
time: 583 us; the launch traced here: 582 us
  waiting for transfers between devices  467 us (80%)
  starting transfers between devices  52 us (9%)
  other arithmetic  33.4 us (6%)
  between operations  14.5 us (2%)
  local copies, waits for them, and re-layouts  12.7 us (2%)
    psum x1, waiting for transfers between devices, local(): gram = lax.psum(local_gram, ('gx', 'gy', 'gz')) / count  433 us
    ppermute x9, starting transfers between devices, padded(): lax.ppermute(lax.slice_in_dim(block, 0, width, axis=dim), axis, backward)  32.1 us
    ppermute x9, waiting for transfers between devices, padded(): lax.ppermute(lax.slice_in_dim(block, 0, width, axis=dim), axis, backward)  25.5 us
    ppermute x9, starting transfers between devices, padded(): lax.ppermute(lax.slice_in_dim(block, block.shape[dim] - width, None, axis...  19.9 us
    another operation x3, other arithmetic, local(): lower = jnp.linalg.cholesky(gram)  12.4 us
  transfers between devices with their start and end apart: 19, of which 11 were waited for; matrix products, arithmetic and copies ran while one was open for 1% of the time, Pallas kernels for 0%

commit v1 on v0

--- a/solution.py
+++ b/solution.py
@@ -64,7 +64,10 @@
     local_gram = jnp.dot(
         stacked, stacked.T, precision=lax.Precision.HIGHEST, preferred_element_type=jnp.float32
     )
-    gram = lax.psum(local_gram, ("gx", "gy", "gz")) / count
+    _place_slots = lambda array_here: lax.psum(
+        lax.psum(array_here, axis_name="gx"), axis_name=("gy", "gz")
+    )
+    gram = _place_slots(local_gram) / count
     lower = jnp.linalg.cholesky(gram)
     basis_next = jax.scipy.linalg.solve_triangular(lower, stacked, lower=True).reshape(
         modes + 1, 3, points

time: 583 us -> 402 us (0.69)
  waiting for transfers between devices: 467 us -> 286 us
    psum x1 -> x2, waiting for transfers between devices: 433 us -> 252 us  [the longest x1 137 us: local(): lax.psum(lax.psum(array_here, axis_name='gx'), axis_name=('gy', 'gz'))]
  transfers between devices with their start and end apart: 19 -> 20, of which waited for: 11 -> 12; matrix products, arithmetic and copies ran while one was open for 1% -> 1% of each run, Pallas kernels for 0% -> 0%
where the time goes in v1:
time: 402 us; the launch traced here: 401 us
  waiting for transfers between devices  286 us (71%)
  starting transfers between devices  52.1 us (13%)
  other arithmetic  33.4 us (8%)
  between operations  14.5 us (4%)
  local copies, waits for them, and re-layouts  12.7 us (3%)
    psum x1, waiting for transfers between devices, local(): lax.psum(lax.psum(array_here, axis_name='gx'), axis_name=('gy', 'gz'))  137 us
    psum x1, waiting for transfers between devices, local(): lax.psum(array_here, axis_name='gx')  115 us
    ppermute x9, starting transfers between devices, padded(): lax.ppermute(lax.slice_in_dim(block, 0, width, axis=dim), axis, backward)  32.1 us
    ppermute x9, waiting for transfers between devices, padded(): lax.ppermute(lax.slice_in_dim(block, 0, width, axis=dim), axis, backward)  25.5 us
    ppermute x9, starting transfers between devices, padded(): lax.ppermute(lax.slice_in_dim(block, block.shape[dim] - width, None, axis...  19.7 us
    another operation x3, other arithmetic, local(): lower = jnp.linalg.cholesky(gram)  12.4 us
    another operation x1, other arithmetic, local(): jax.scipy.linalg.solve_triangular(lower, stacked, lower=True)  9.81 us
    ppermute x9, waiting for transfers between devices, padded(): lax.ppermute(lax.slice_in_dim(block, block.shape[dim] - width, None, axis...  8.92 us
  transfers between devices with their start and end apart: 20, of which 12 were waited for; matrix products, arithmetic and copies ran while one was open for 1% of the time, Pallas kernels for 0%

profile of v1, /device:TPU:1, one launch (start us, length us, event | category | flops | bytes accessed | tf_op | source)
XLA Modules:
  0.0 401.5 jit_solution(337048168244483214)
XLA Ops:
  8.3 3.9 collective-permute-start
  14.4 2.2 collective-permute-done.1
  17.5 11.1 %collective-permute-start.2 = (f32[4,1,18,128]{3,2,1,0:T(8,128)S(1)}, f32[4,1,18,128]{3,2,1,0:T(8,128)S(1)}, u32[]{:S(2)}, u32[]{:S(2)}) collective-permute-start(f32[4,1,18,128]{3,2,1,0:T(8,128)S(1)} %get-tuple-element.41), channel_id=1, source_target_pairs={{32,0},{64,32},{96,64},{128,96},{160,128},{192,160},{224,192},{256... | collective-permute-start | bytes 110600 | tf_op jit(solution)/shard_map/ppermute | solution.py:22
  31.2 3.4 collective-permute-done.3
  35.9 3.5 collective-permute-start.4
  42.2 5.2 %collective-permute-done.4 = f32[4,10,18,1]{3,2,1,0:T(8,128)S(1)} collective-permute-done((f32[4,10,18,1]{3,2,1,0:T(8,128)S(1)}, f32[4,10,18,1]{3,2,1,0:T(8,128)S(1)}, u32[]{:S(2)}, u32[]{:S(2)}) %collective-permute-start.4) | collective-permute-done | bytes 2912 | tf_op jit(solution)/shard_map/ppermute | solution.py:22
  50.4 3.1 collective-permute-start.6
  54.9 3.1 collective-permute-done.7
  60.0 3.4 collective-permute-start.9
  63.4 2.6 collective-permute-done.9
  66.3 4.2 %collective-permute-start.10 = (f32[4,10,18,1]{3,2,1,0:T(8,128)S(1)}, f32[4,10,18,1]{3,2,1,0:T(8,128)S(1)}, u32[]{:S(2)}, u32[]{:S(2)}) collective-permute-start(f32[4,10,18,1]{3,2,1,0:T(8,128)S(1)} %get-tuple-element.29), channel_id=1, source_target_pairs={{1,0},{2,1},{3,2},{4,3},{5,4},{6,5},{7,6},{0,7},{9,8},{10,9},{11,1... | collective-permute-start | bytes 8648 | tf_op jit(solution)/shard_map/ppermute | solution.py:22
  70.7 6.5 %collective-permute-done.10 = f32[4,10,18,1]{3,2,1,0:T(8,128)S(1)} collective-permute-done((f32[4,10,18,1]{3,2,1,0:T(8,128)S(1)}, f32[4,10,18,1]{3,2,1,0:T(8,128)S(1)}, u32[]{:S(2)}, u32[]{:S(2)}) %collective-permute-start.10) | collective-permute-done | bytes 2912 | tf_op jit(solution)/shard_map/ppermute | solution.py:22
  77.9 2.8 collective-permute-start.12
  82.2 3.0 collective-permute-done.13
  87.1 3.4 collective-permute-start.15
  90.5 2.6 collective-permute-done.15
  93.4 5.4 %collective-permute-start.16 = (f32[4,10,18,1]{3,2,1,0:T(8,128)S(1)}, f32[4,10,18,1]{3,2,1,0:T(8,128)S(1)}, u32[]{:S(2)}, u32[]{:S(2)}) collective-permute-start(f32[4,10,18,1]{3,2,1,0:T(8,128)S(1)} %get-tuple-element.27), channel_id=1, source_target_pairs={{1,0},{2,1},{3,2},{4,3},{5,4},{6,5},{7,6},{0,7},{9,8},{10,9},{11,1... | collective-permute-start | bytes 8648 | tf_op jit(solution)/shard_map/ppermute | solution.py:22
  99.0 5.4 %collective-permute-done.16 = f32[4,10,18,1]{3,2,1,0:T(8,128)S(1)} collective-permute-done((f32[4,10,18,1]{3,2,1,0:T(8,128)S(1)}, f32[4,10,18,1]{3,2,1,0:T(8,128)S(1)}, u32[]{:S(2)}, u32[]{:S(2)}) %collective-permute-start.16) | collective-permute-done | bytes 2912 | tf_op jit(solution)/shard_map/ppermute | solution.py:22
  105.3 4.7 %copy.16 = f32[3,8,16,128]{0,3,2,1:T(8,128)} copy(f32[3,8,16,128]{3,2,1,0:T(8,128)S(1)} %slice.406) | data formatting | bytes 393216 | tf_op jit(solution)/shard_map/slice | solution.py:61
  110.1 4.1 %gather_fusion = f32[256,3]{1,0:T(8,128)S(1)} fusion(f32[3,16384]{0,1:T(8,128)} %bitcast.47, s32[1024]{0:T(1024)S(1)} %pad_clamp_fusion), kind=kCustom, calls=%fused_computation | custom fusion | bytes 7168 | tf_op jit(solution)/shard_map/jit(_take)/gather | solution.py:62
  115.8 115.1 %all-reduce.3.cloned.1.call-done = f32[128,128]{0,1:T(8,128)} async-done(((f32[128,128]{0,1:T(8,128)}), f32[128,128]{0,1:T(8,128)}) %all-reduce.3.cloned.1.call-update) | async-done | bytes 65552 | tf_op jit(solution)/shard_map/psum | solution.py:68
  231.1 136.8 %all-reduce.5.cloned.1.call-done = f32[128,128]{0,1:T(8,128)} async-done(((f32[128,128]{0,1:T(8,128)}), f32[128,128]{0,1:T(8,128)}) %all-reduce.5.cloned.1.call-update) | async-done | bytes 65552 | tf_op jit(solution)/shard_map/psum | solution.py:67
  369.8 11.7 %cholesky.16 = f32[128,128]{1,0:T(8,128)S(1)} custom-call(f32[128,128]{1,0:T(8,128)S(1)} %fusion.57), custom_call_target="Cholesky" | custom-call | tf_op jit(solution)/shard_map/jit(cholesky)/cholesky | solution.py:71
  382.8 9.8 %custom-call.7 = f32[1,128,128]{1,2,0:T(8,128)S(1)} custom-call(f32[1,128,128]{2,1,0:T(8,128)S(1)} %get-tuple-element.70), custom_call_target="InvertDiagBlocksLowerTriangular" | custom-call | tf_op jit(solution)/shard_map/jit(_solve_triangular)/triangular_solve | solution.py:72
  (82 shorter events, 29.5 us)
Async XLA Ops:
  7.2 43.2 %copy-start = (f32[4,8,16,128]{3,2,1,0:T(8,128)S(1)}, f32[4,8,16,128]{3,2,1,0:T(8,128)}, u32[]{:S(2)}) copy-start(f32[4,8,16,128]{3,2,1,0:T(8,128)} %param.6) | copy-start | bytes 786436
  7.2 47.7 %copy-start.4 = (s32[256]{0:T(256)S(1)}, s32[256]{0:T(256)}, u32[]{:S(2)}) copy-start(s32[256]{0:T(256)} %param.8) | copy-start | bytes 3076
  7.2 223.7 %all-reduce.3.cloned.1.call-start = ((), (), s32[]{:S(2)}) async-start(), calls=%async_computation | async-start | bytes 131072 | tf_op jit(solution)/shard_map/psum | solution.py:68
  8.3 6.2 %collective-permute-start = (f32[4,8,1,128]{3,2,1,0:T(1,128)S(1)}, f32[4,8,1,128]{3,2,1,0:T(1,128)S(1)}, u32[]{:S(2)}, u32[]{:S(2)}) collective-permute-start(f32[4,8,1,128]{3,2,1,0:T(1,128)S(1)} %get-tuple-element.67), channel_id=1, source_target_pairs={{0,8},{8,16},{16,24},{1,9},{9,17},{17,25},{2,10},{10,18},{18,26},{... | collective-permute-start | bytes 49160 | tf_op jit(solution)/shard_map/ppermute | solution.py:19
  12.2 4.5 %collective-permute-start.1 = (f32[4,8,1,128]{3,2,1,0:T(1,128)S(1)}, f32[4,8,1,128]{3,2,1,0:T(1,128)S(1)}, u32[]{:S(2)}, u32[]{:S(2)}) collective-permute-start(f32[4,8,1,128]{3,2,1,0:T(1,128)S(1)} %get-tuple-element.68), channel_id=1, source_target_pairs={{8,0},{16,8},{24,16},{9,1},{17,9},{25,17},{10,2},{18,10},{26,18},{... | collective-permute-start | bytes 49160 | tf_op jit(solution)/shard_map/ppermute | solution.py:22
  17.5 13.7 %collective-permute-start.2 = (f32[4,1,18,128]{3,2,1,0:T(8,128)S(1)}, f32[4,1,18,128]{3,2,1,0:T(8,128)S(1)}, u32[]{:S(2)}, u32[]{:S(2)}) collective-permute-start(f32[4,1,18,128]{3,2,1,0:T(8,128)S(1)} %get-tuple-element.41), channel_id=1, source_target_pairs={{32,0},{64,32},{96,64},{128,96},{160,128},{192,160},{224,192},{256... | collective-permute-start | bytes 110600 | tf_op jit(solution)/shard_map/ppermute | solution.py:22
  28.6 6.0 %collective-permute-start.3 = (f32[4,1,18,128]{3,2,1,0:T(8,128)S(1)}, f32[4,1,18,128]{3,2,1,0:T(8,128)S(1)}, u32[]{:S(2)}, u32[]{:S(2)}) collective-permute-start(f32[4,1,18,128]{3,2,1,0:T(8,128)S(1)} %get-tuple-element.40), channel_id=1, source_target_pairs={{0,32},{32,64},{64,96},{96,128},{128,160},{160,192},{192,224},{224... | collective-permute-start | bytes 110600 | tf_op jit(solution)/shard_map/ppermute | solution.py:19
  35.7 41.9 %copy-start.3 = (f32[3]{0:T(128)S(1)}, f32[3]{0:T(128)}, u32[]{:S(2)}) copy-start(f32[3]{0:T(128)} %constant.80.clone) | copy-start | bytes 40
  35.9 11.5 %collective-permute-start.4 = (f32[4,10,18,1]{3,2,1,0:T(8,128)S(1)}, f32[4,10,18,1]{3,2,1,0:T(8,128)S(1)}, u32[]{:S(2)}, u32[]{:S(2)}) collective-permute-start(f32[4,10,18,1]{3,2,1,0:T(8,128)S(1)} %get-tuple-element.31), channel_id=1, source_target_pairs={{1,0},{2,1},{3,2},{4,3},{5,4},{6,5},{7,6},{0,7},{9,8},{10,9},{11,1... | collective-permute-start | bytes 8648 | tf_op jit(solution)/shard_map/ppermute | solution.py:22
  39.4 8.0 %collective-permute-start.5 = (f32[4,10,18,1]{3,2,1,0:T(8,128)S(1)}, f32[4,10,18,1]{3,2,1,0:T(8,128)S(1)}, u32[]{:S(2)}, u32[]{:S(2)}) collective-permute-start(f32[4,10,18,1]{3,2,1,0:T(8,128)S(1)} %get-tuple-element.32), channel_id=1, source_target_pairs={{0,1},{1,2},{2,3},{3,4},{4,5},{5,6},{6,7},{7,0},{8,9},{9,10},{10,1... | collective-permute-start | bytes 8648 | tf_op jit(solution)/shard_map/ppermute | solution.py:19
  50.4 4.5 %collective-permute-start.6 = (f32[4,8,1,128]{3,2,1,0:T(1,128)S(1)}, f32[4,8,1,128]{3,2,1,0:T(1,128)S(1)}, u32[]{:S(2)}, u32[]{:S(2)}) collective-permute-start(f32[4,8,1,128]{3,2,1,0:T(1,128)S(1)} %get-tuple-element.58), channel_id=1, source_target_pairs={{0,8},{8,16},{16,24},{1,9},{9,17},{17,25},{2,10},{10,18},{18,26},{... | collective-permute-start | bytes 49160 | tf_op jit(solution)/shard_map/ppermute | solution.py:19
  53.6 4.5 %collective-permute-start.7 = (f32[4,8,1,128]{3,2,1,0:T(1,128)S(1)}, f32[4,8,1,128]{3,2,1,0:T(1,128)S(1)}, u32[]{:S(2)}, u32[]{:S(2)}) collective-permute-start(f32[4,8,1,128]{3,2,1,0:T(1,128)S(1)} %get-tuple-element.59), channel_id=1, source_target_pairs={{8,0},{16,8},{24,16},{9,1},{17,9},{25,17},{10,2},{18,10},{26,18},{... | collective-permute-start | bytes 49160 | tf_op jit(solution)/shard_map/ppermute | solution.py:22
  58.1 5.3 %collective-permute-start.8 = (f32[4,1,18,128]{3,2,1,0:T(8,128)S(1)}, f32[4,1,18,128]{3,2,1,0:T(8,128)S(1)}, u32[]{:S(2)}, u32[]{:S(2)}) collective-permute-start(f32[4,1,18,128]{3,2,1,0:T(8,128)S(1)} %get-tuple-element.38), channel_id=1, source_target_pairs={{32,0},{64,32},{96,64},{128,96},{160,128},{192,160},{224,192},{256... | collective-permute-start | bytes 110600 | tf_op jit(solution)/shard_map/ppermute | solution.py:22
  60.0 6.0 %collective-permute-start.9 = (f32[4,1,18,128]{3,2,1,0:T(8,128)S(1)}, f32[4,1,18,128]{3,2,1,0:T(8,128)S(1)}, u32[]{:S(2)}, u32[]{:S(2)}) collective-permute-start(f32[4,1,18,128]{3,2,1,0:T(8,128)S(1)} %get-tuple-element.37), channel_id=1, source_target_pairs={{0,32},{32,64},{64,96},{96,128},{128,160},{160,192},{192,224},{224... | collective-permute-start | bytes 110600 | tf_op jit(solution)/shard_map/ppermute | solution.py:19
  66.3 10.9 %collective-permute-start.10 = (f32[4,10,18,1]{3,2,1,0:T(8,128)S(1)}, f32[4,10,18,1]{3,2,1,0:T(8,128)S(1)}, u32[]{:S(2)}, u32[]{:S(2)}) collective-permute-start(f32[4,10,18,1]{3,2,1,0:T(8,128)S(1)} %get-tuple-element.29), channel_id=1, source_target_pairs={{1,0},{2,1},{3,2},{4,3},{5,4},{6,5},{7,6},{0,7},{9,8},{10,9},{11,1... | collective-permute-start | bytes 8648 | tf_op jit(solution)/shard_map/ppermute | solution.py:22
  70.5 6.6 %collective-permute-start.11 = (f32[4,10,18,1]{3,2,1,0:T(8,128)S(1)}, f32[4,10,18,1]{3,2,1,0:T(8,128)S(1)}, u32[]{:S(2)}, u32[]{:S(2)}) collective-permute-start(f32[4,10,18,1]{3,2,1,0:T(8,128)S(1)} %get-tuple-element.30), channel_id=1, source_target_pairs={{0,1},{1,2},{2,3},{3,4},{4,5},{5,6},{6,7},{7,0},{8,9},{9,10},{10,1... | collective-permute-start | bytes 8648 | tf_op jit(solution)/shard_map/ppermute | solution.py:19
  77.9 4.3 %collective-permute-start.12 = (f32[4,8,1,128]{3,2,1,0:T(1,128)S(1)}, f32[4,8,1,128]{3,2,1,0:T(1,128)S(1)}, u32[]{:S(2)}, u32[]{:S(2)}) collective-permute-start(f32[4,8,1,128]{3,2,1,0:T(1,128)S(1)} %get-tuple-element.49), channel_id=1, source_target_pairs={{0,8},{8,16},{16,24},{1,9},{9,17},{17,25},{2,10},{10,18},{18,26},{... | collective-permute-start | bytes 49160 | tf_op jit(solution)/shard_map/ppermute | solution.py:19
  80.7 4.5 %collective-permute-start.13 = (f32[4,8,1,128]{3,2,1,0:T(1,128)S(1)}, f32[4,8,1,128]{3,2,1,0:T(1,128)S(1)}, u32[]{:S(2)}, u32[]{:S(2)}) collective-permute-start(f32[4,8,1,128]{3,2,1,0:T(1,128)S(1)} %get-tuple-element.50), channel_id=1, source_target_pairs={{8,0},{16,8},{24,16},{9,1},{17,9},{25,17},{10,2},{18,10},{26,18},{... | collective-permute-start | bytes 49160 | tf_op jit(solution)/shard_map/ppermute | solution.py:22
  85.2 5.3 %collective-permute-start.14 = (f32[4,1,18,128]{3,2,1,0:T(8,128)S(1)}, f32[4,1,18,128]{3,2,1,0:T(8,128)S(1)}, u32[]{:S(2)}, u32[]{:S(2)}) collective-permute-start(f32[4,1,18,128]{3,2,1,0:T(8,128)S(1)} %get-tuple-element.35), channel_id=1, source_target_pairs={{32,0},{64,32},{96,64},{128,96},{160,128},{192,160},{224,192},{256... | collective-permute-start | bytes 110600 | tf_op jit(solution)/shard_map/ppermute | solution.py:22
  87.1 6.0 %collective-permute-start.15 = (f32[4,1,18,128]{3,2,1,0:T(8,128)S(1)}, f32[4,1,18,128]{3,2,1,0:T(8,128)S(1)}, u32[]{:S(2)}, u32[]{:S(2)}) collective-permute-start(f32[4,1,18,128]{3,2,1,0:T(8,128)S(1)} %get-tuple-element.34), channel_id=1, source_target_pairs={{0,32},{32,64},{64,96},{96,128},{128,160},{160,192},{192,224},{224... | collective-permute-start | bytes 110600 | tf_op jit(solution)/shard_map/ppermute | solution.py:19
  93.4 11.0 %collective-permute-start.16 = (f32[4,10,18,1]{3,2,1,0:T(8,128)S(1)}, f32[4,10,18,1]{3,2,1,0:T(8,128)S(1)}, u32[]{:S(2)}, u32[]{:S(2)}) collective-permute-start(f32[4,10,18,1]{3,2,1,0:T(8,128)S(1)} %get-tuple-element.27), channel_id=1, source_target_pairs={{1,0},{2,1},{3,2},{4,3},{5,4},{6,5},{7,6},{0,7},{9,8},{10,9},{11,1... | collective-permute-start | bytes 8648 | tf_op jit(solution)/shard_map/ppermute | solution.py:22
  98.9 5.8 %collective-permute-start.17 = (f32[4,10,18,1]{3,2,1,0:T(8,128)S(1)}, f32[4,10,18,1]{3,2,1,0:T(8,128)S(1)}, u32[]{:S(2)}, u32[]{:S(2)}) collective-permute-start(f32[4,10,18,1]{3,2,1,0:T(8,128)S(1)} %get-tuple-element.28), channel_id=1, source_target_pairs={{0,1},{1,2},{2,3},{3,4},{4,5},{5,6},{6,7},{7,0},{8,9},{9,10},{10,1... | collective-permute-start | bytes 8648 | tf_op jit(solution)/shard_map/ppermute | solution.py:19
  105.3 289.4 %copy-start.2 = (f32[4,8,16,128]{3,2,1,0:T(8,128)}, f32[4,8,16,128]{3,2,1,0:T(8,128)S(1)}, u32[]{:S(2)}) copy-start(f32[4,8,16,128]{3,2,1,0:T(8,128)S(1)} %fusion.15) | copy-start | bytes 786436
  115.4 252.6 %all-reduce.5.cloned.1.call-start = ((), (), s32[]{:S(2)}) async-start(), calls=%async_computation.1 | async-start | bytes 131072 | tf_op jit(solution)/shard_map/psum | solution.py:67
  (1 other events, 39.8 us)
Sparse Core Ops, SparseCore 0:
  115.5 115.3 all-reduce.2
  234.5 133.4 all-reduce.4
